TPU v7x, 32 devices: a whole 2x2x4 slice. The times are simulated.
32 devices in a mesh: front: 16 (over z, y, x), panel: 2 (over core).
Axes of the slice: x: 2, y: 2, z: 4, core: 2. Of those that a mesh axis runs over, the one named last changes fastest.
Arguments:
- sep_factor: bfloat16 [16384, 1024], P(('front', 'panel')), may hold values from -3 to 3, as said below
- coup_factor: bfloat16 [32768, 1024], P(('front', 'panel')), may hold values from -0.1875 to 0.1875
- coup_list: int32 [16, 16], replicated, may hold values from -1 to 15, as said below
- slot_tiles: int32 [16, 16], replicated, may hold values from 0 to 255, as said below
- anc_tiles: bfloat16 [32768, 128], P('front'), may hold values from -50 to 50
Outputs:
- selected_inverse: float32 [16384, 1024], P(('front', 'panel'))
- variances: float32 [16384], P(('front', 'panel'))
Inputs may be any that keep to these rules, and one draw needn't show every extreme that they name: `sep_factor`: each front's block of 1024 rows is lower triangular with a diagonal of 1 or more. `coup_list`: a front's entries name distinct blocks; live entries come first and the rest are -1; every front has 4 or more live entries and some front has 16. `slot_tiles`: every strip id of 0 to 255 appears in exactly one slot; every group holds exactly one strip of each block row.
All inputs are finite; a program needn't handle non-finite values.
Results may differ from a plain program's by a relative error of at most 0.0056.
Values may be sent and summed in bfloat16 or wider, within the bound.
A program may use at most 128 MiB of HBM per device.

v0:
```python
import jax
import jax.numpy as jnp
from jax import lax
from jax.sharding import PartitionSpec as P


def on_device(sep_factor, coup_factor, coup_list, slot_tiles, anc_tiles):
    panels = lax.axis_size("panel")
    groups = lax.axis_size("front")
    panel_rank = lax.axis_index("panel")
    my_group = lax.axis_index("front")
    sep_rows = sep_factor.shape[0]
    sep_width = sep_factor.shape[1]
    tile_edge = anc_tiles.shape[1]
    strips_owned = slot_tiles.shape[1]
    strip_rows = anc_tiles.shape[0] // strips_owned
    strip_count = tile_edge // strip_rows
    list_width = coup_list.shape[1]
    row_blocks = list_width // panels
    first_block = panel_rank * row_blocks
    lower_full = lax.all_gather(sep_factor, "panel", axis=0, tiled=True).astype(jnp.float32)
    identity = jnp.eye(sep_width, dtype=jnp.float32)
    inverse = lax.linalg.triangular_solve(lower_full, identity, left_side=True, lower=True)
    own_columns = lax.dynamic_slice_in_dim(inverse, panel_rank * sep_rows, sep_rows, 1)
    inverse_square = jnp.dot(own_columns.T, inverse, precision=lax.Precision.HIGHEST)
    inverse_half = inverse.astype(jnp.bfloat16)
    own_list = coup_list[my_group]
    live_blocks = own_list >= 0
    live_mine = lax.dynamic_slice_in_dim(live_blocks, first_block, row_blocks)
    row_live = jnp.repeat(live_mine, tile_edge)
    coupling = jnp.where(row_live[:, None], coup_factor, jnp.zeros_like(coup_factor))
    wide_mine = jnp.dot(coupling, inverse_half, preferred_element_type=jnp.float32).astype(
        jnp.bfloat16
    )
    wide_full = lax.all_gather(wide_mine, "panel", axis=0, tiled=True)
    mine_ids = slot_tiles[my_group]
    mine_rows = mine_ids // groups
    mine_cols = mine_ids % groups // strip_count
    wanted = lax.dynamic_slice_in_dim(coup_list, first_block, row_blocks, 1)
    in_list = jnp.any(coup_list[:, None, :] == mine_cols[None, :, None], axis=2)
    chosen = (mine_rows[None, None, :] == wanted[:, :, None]) & in_list[:, None, :]
    strip_stack = anc_tiles.reshape(strips_owned, strip_rows, tile_edge)
    outgoing = jnp.einsum(
        "gks,sxy->gkxy",
        chosen.astype(jnp.bfloat16),
        strip_stack,
        preferred_element_type=jnp.float32,
    ).astype(jnp.bfloat16)
    outgoing = outgoing.reshape(groups, row_blocks * strip_rows, tile_edge)
    incoming = lax.all_to_all(outgoing, "front", split_axis=0, concat_axis=0, tiled=True)
    incoming = incoming.reshape(groups, row_blocks, strip_rows, tile_edge)
    their_rows = slot_tiles // groups
    their_place = slot_tiles % groups
    their_cols = their_place // strip_count
    their_parts = their_place % strip_count
    wanted_mine = lax.dynamic_slice_in_dim(own_list, first_block, row_blocks)
    row_hit = (their_rows[:, None, :] == wanted_mine[None, :, None]).astype(jnp.float32)
    col_hit = (their_cols[:, :, None] == own_list[None, None, :]).astype(jnp.float32)
    part_index = jnp.arange(strip_count, dtype=jnp.int32)
    part_hit = (their_parts[:, :, None] == part_index[None, None, :]).astype(jnp.float32)
    placing = jnp.einsum("fks,fsq,fsb->fkqb", row_hit, part_hit, col_hit).astype(jnp.bfloat16)
    sigma_rows = jnp.einsum(
        "fkqb,fkxy->kqxby", placing, incoming, preferred_element_type=jnp.float32
    ).astype(jnp.bfloat16)
    sigma_rows = sigma_rows.reshape(row_blocks * tile_edge, list_width * tile_edge)
    carried = jnp.dot(sigma_rows, wide_full, preferred_element_type=jnp.float32).astype(
        jnp.bfloat16
    )
    summed = lax.psum_scatter(
        lax.dot_general(
            wide_mine, carried, (((0,), (0,)), ((), ())), preferred_element_type=jnp.float32
        ),
        "panel",
        scatter_dimension=0,
        tiled=True,
    )
    selected = inverse_square + summed
    diagonal_block = lax.dynamic_slice_in_dim(selected, panel_rank * sep_rows, sep_rows, 1)
    variances = jnp.diagonal(diagonal_block)
    return (selected, variances)


def solution(mesh):
    placed = (P(("front", "panel"), None), P(("front", "panel"), None), P(), P(), P("front", None))
    return jax.shard_map(
        on_device,
        mesh=mesh,
        in_specs=placed,
        out_specs=(P(("front", "panel"), None), P(("front", "panel"))),
        check_vma=False,
    )
```

profile of v0, /device:TPU:0, one launch (start us, length us, event | category | flops | bytes accessed | tf_op | source)
XLA Modules:
  0.0 226.8 jit_solution(5698630347051967437)
XLA Ops:
  7.2 0.7 all-gather.3.cloned.1.call-update
  7.9 0.7 and_select_fusion
  8.6 0.8 constant_dynamic-slice_fusion.2
  9.4 1.1 compare_reduce_fusion
  10.5 0.7 and_select_fusion.1
  11.2 2.3 %convolution_convert_fusion.1 = bf16[16,8,128,128]{3,1,2,0:T(8,128)(2,1)S(1)} fusion(bf16[16,128,128]{2,1,0:T(8,128)(2,1)} %bitcast.108, s32[16,8]{1,0:T(8,128)S(1)} %constant_dynamic-slice_fusion.2, s32[16]{0:T(128)S(1)} %and_select_fusion.1, pred[16,16]{1,0:T(8,128)(4,1)S(1)} %compare_reduce_fusion), kind=kOutput, calls=%fused_computation.10 | convolution fusion | flops 69210112 | bytes 4719424 | tf_op jit(solution)/shard_map/gks,sxy->gkxy/dot_general | solution.py:43
  13.5 3.2 %copy.12 = bf16[16,8,128,128]{3,2,1,0:T(8,128)(2,1)} copy(bf16[16,8,128,128]{3,1,2,0:T(8,128)(2,1)S(1)} %convolution_convert_fusion.1) | data formatting | bytes 8388608 | tf_op jit(solution)/shard_map/convert_element_type | solution.py:48
  16.8 8.4 %all-to-all-start = ((bf16[16,1024,128]{2,1,0:T(8,128)(2,1)}), bf16[16,1024,128]{2,1,0:T(8,128)(2,1)}, u32[]{:S(2)}, u32[]{:S(2)}) async-start(bf16[16,1024,128]{2,1,0:T(8,128)(2,1)} %bitcast.105), calls=%async_computation | async-start | bytes 8388608 | tf_op jit(solution)/shard_map/all_to_all | solution.py:50
  25.2 0.7 broadcast_compare_fusion
  26.3 2.5 %fusion.40 = f32[1024,1024]{1,0:T(8,128)} fusion(), kind=kLoop, calls=%fused_computation.45 | loop fusion | flops 2097152 | bytes 4194304 | tf_op jit(solution)/shard_map/convert_element_type | solution.py:22
  28.9 4.1 %convert_select_fusion = f32[1024,1024]{1,0:T(8,128)} fusion(bf16[1024,1024]{1,0:T(8,128)(2,1)} %all-gather.3.cloned.1.call-done), kind=kLoop, calls=%fused_computation.7 | loop fusion | flops 3145728 | bytes 6291456 | tf_op jit(solution)/shard_map/triangular_solve | solution.py:23
  33.0 23.3 %while.1 = (s32[]{:T(128)}, f32[1024,1024]{1,0:T(8,128)}, s32[8,2]{0,1:T(2,128)S(1)}, f32[8,128,128]{2,1,0:T(8,128)S(1)}, s32[]{:T(128)}) while((s32[]{:T(128)}, f32[1024,1024]{1,0:T(8,128)}, s32[8,2]{0,1:T(2,128)S(1)}, f32[8,128,128]{2,1,0:T(8,128)S(1)}, s32[]{:T(128)}) %tuple.48), condition=%wide.while_cond, body=%wide.while_body.sunk | while | flops 2 | bytes 131181 | solution.py:23
  33.6 2.3 %bitcast_dynamic-update-slice_fusion.2 = f32[8,128,128]{2,1,0:T(8,128)S(1)} fusion(f32[8,128,128]{2,1,0:T(8,128)S(1)} %get-tuple-element.92, s32[]{:T(128)} %get-tuple-element.89, f32[1024,1024]{1,0:T(8,128)} %get-tuple-element.95, s32[]{:T(128)} %bitcast.102, s32[]{:T(128)} %bitcast.103), kind=kLoop, calls=%fused_computation.1.clone.1 | loop fusion | bytes 131084 | tf_op jit(solution)/shard_map/triangular_solve
  36.5 2.3 %bitcast_dynamic-update-slice_fusion.2 = f32[8,128,128]{2,1,0:T(8,128)S(1)} fusion(f32[8,128,128]{2,1,0:T(8,128)S(1)} %get-tuple-element.92, s32[]{:T(128)} %get-tuple-element.89, f32[1024,1024]{1,0:T(8,128)} %get-tuple-element.95, s32[]{:T(128)} %bitcast.102, s32[]{:T(128)} %bitcast.103), kind=kLoop, calls=%fused_computation.1.clone.1 | loop fusion | bytes 131084 | tf_op jit(solution)/shard_map/triangular_solve
  38.9 0.5 fusion.111
  39.4 2.3 %bitcast_dynamic-update-slice_fusion.2 = f32[8,128,128]{2,1,0:T(8,128)S(1)} fusion(f32[8,128,128]{2,1,0:T(8,128)S(1)} %get-tuple-element.92, s32[]{:T(128)} %get-tuple-element.89, f32[1024,1024]{1,0:T(8,128)} %get-tuple-element.95, s32[]{:T(128)} %bitcast.102, s32[]{:T(128)} %bitcast.103), kind=kLoop, calls=%fused_computation.1.clone.1 | loop fusion | bytes 131084 | tf_op jit(solution)/shard_map/triangular_solve
  41.8 0.5 fusion.111
  42.3 2.3 %bitcast_dynamic-update-slice_fusion.2 = f32[8,128,128]{2,1,0:T(8,128)S(1)} fusion(f32[8,128,128]{2,1,0:T(8,128)S(1)} %get-tuple-element.92, s32[]{:T(128)} %get-tuple-element.89, f32[1024,1024]{1,0:T(8,128)} %get-tuple-element.95, s32[]{:T(128)} %bitcast.102, s32[]{:T(128)} %bitcast.103), kind=kLoop, calls=%fused_computation.1.clone.1 | loop fusion | bytes 131084 | tf_op jit(solution)/shard_map/triangular_solve
  44.7 0.5 fusion.111
  45.2 2.3 %bitcast_dynamic-update-slice_fusion.2 = f32[8,128,128]{2,1,0:T(8,128)S(1)} fusion(f32[8,128,128]{2,1,0:T(8,128)S(1)} %get-tuple-element.92, s32[]{:T(128)} %get-tuple-element.89, f32[1024,1024]{1,0:T(8,128)} %get-tuple-element.95, s32[]{:T(128)} %bitcast.102, s32[]{:T(128)} %bitcast.103), kind=kLoop, calls=%fused_computation.1.clone.1 | loop fusion | bytes 131084 | tf_op jit(solution)/shard_map/triangular_solve
  48.2 2.3 %bitcast_dynamic-update-slice_fusion.2 = f32[8,128,128]{2,1,0:T(8,128)S(1)} fusion(f32[8,128,128]{2,1,0:T(8,128)S(1)} %get-tuple-element.92, s32[]{:T(128)} %get-tuple-element.89, f32[1024,1024]{1,0:T(8,128)} %get-tuple-element.95, s32[]{:T(128)} %bitcast.102, s32[]{:T(128)} %bitcast.103), kind=kLoop, calls=%fused_computation.1.clone.1 | loop fusion | bytes 131084 | tf_op jit(solution)/shard_map/triangular_solve
  51.1 2.3 %bitcast_dynamic-update-slice_fusion.2 = f32[8,128,128]{2,1,0:T(8,128)S(1)} fusion(f32[8,128,128]{2,1,0:T(8,128)S(1)} %get-tuple-element.92, s32[]{:T(128)} %get-tuple-element.89, f32[1024,1024]{1,0:T(8,128)} %get-tuple-element.95, s32[]{:T(128)} %bitcast.102, s32[]{:T(128)} %bitcast.103), kind=kLoop, calls=%fused_computation.1.clone.1 | loop fusion | bytes 131084 | tf_op jit(solution)/shard_map/triangular_solve
  54.0 2.2 bitcast_dynamic-update-slice_fusion.2
  56.2 78.8 %custom-call.3 = f32[8,128,128]{1,2,0:T(8,128)S(1)} custom-call(f32[8,128,128]{2,1,0:T(8,128)S(1)} %get-tuple-element.9), custom_call_target="InvertDiagBlocksLowerTriangular" | custom-call | tf_op jit(solution)/shard_map/triangular_solve | solution.py:23
  135.6 1.9 convolution_subtract_fusion.4
  137.5 0.7 constant_dynamic-update-slice_fusion.16
  138.2 1.6 convolution_subtract_fusion
  139.9 0.7 constant_dynamic-update-slice_fusion.15
  140.6 2.0 fusion.33
  142.7 0.7 constant_dynamic-update-slice_fusion.14
  143.4 2.2 fusion.36
  145.6 0.7 constant_dynamic-update-slice_fusion.13
  146.4 2.6 %convolution_subtract_fusion.2 = f32[128,1024]{1,0:T(8,128)S(1)} fusion(f32[640,1024]{1,0:T(8,128)S(1)} %get-tuple-element.32, f32[1024,1024]{1,0:T(8,128)S(1)} %copy-done, f32[1024,1024]{1,0:T(8,128)} %get-tuple-element.104), kind=kOutput, calls=%fused_computation.40 | convolution fusion | flops 1006764032 | bytes 3997696 | tf_op jit(solution)/shard_map/triangular_solve | solution.py:23
  149.0 0.7 constant_dynamic-update-slice_fusion.12
  149.7 2.8 %convolution_subtract_fusion.1 = f32[128,1024]{1,0:T(8,128)S(1)} fusion(f32[768,1024]{1,0:T(8,128)S(1)} %get-tuple-element.28, f32[1024,1024]{1,0:T(8,128)S(1)} %copy-done, f32[1024,1024]{1,0:T(8,128)} %get-tuple-element.104), kind=kOutput, calls=%fused_computation.37 | convolution fusion | flops 1208090624 | bytes 4587520 | tf_op jit(solution)/shard_map/triangular_solve | solution.py:23
  152.5 0.6 constant_dynamic-update-slice_fusion.11
  153.2 3.5 %convolution_subtract_fusion.3 = f32[128,1024]{1,0:T(8,128)S(1)} fusion(f32[896,1024]{1,0:T(8,128)S(1)} %get-tuple-element.24, f32[1024,1024]{1,0:T(8,128)S(1)} %copy-done, f32[1024,1024]{1,0:T(8,128)} %get-tuple-element.104), kind=kOutput, calls=%fused_computation.41 | convolution fusion | flops 1409417216 | bytes 5177344 | tf_op jit(solution)/shard_map/triangular_solve | solution.py:23
  156.6 0.6 convolution_dynamic-update-slice_fusion
  157.3 2.0 copy-done.1
  159.3 3.7 %fusion.19 = bf16[1024,1024]{1,0:T(8,128)(2,1)} fusion(f32[1024,1024]{1,0:T(8,128)S(1)} %convolution_dynamic-update-slice_fusion, bf16[1024,1024]{1,0:T(8,128)(2,1)S(1)} %copy-done.5, pred[1024]{0:T(1024)(128)(4,1)S(1)} %broadcast_bitcast_fusion), kind=kOutput, calls=%fused_computation.27 | convolution fusion | flops 2150629376 | bytes 8389632 | tf_op jit(solution)/shard_map/dot_general | solution.py:32
  163.0 0.8 dynamic-slice_bitcast_fusion
  164.1 4.9 %copy.13 = bf16[16,1024,128]{2,0,1:T(8,128)(2,1)S(1)} copy(bf16[16,1024,128]{2,1,0:T(8,128)(2,1)} %all-to-all-done) | data formatting | bytes 8388608 | tf_op jit(solution)/shard_map/all_to_all | solution.py:50
  169.0 2.9 %convolution_convert_fusion = bf16[8,128,128,16]{2,3,1,0:T(8,128)(2,1)} fusion(bf16[16,8,128,128]{3,0,2,1:T(8,128)(2,1)S(1)} %bitcast.106, bf16[16,8,16,1]{2,1,0,3:T(8,128)(2,1)S(1)} %fusion.39), kind=kOutput, calls=%fused_computation.9 | convolution fusion | flops 69206016 | bytes 8392704 | tf_op jit(solution)/shard_map/fkqb,fkxy->kqxby/dot_general | solution.py:62
  171.9 6.2 %all-gather.5.cloned.1.call-done = bf16[2048,1024]{1,0:T(8,128)(2,1)} async-done(((bf16[1024,1024]{1,0:T(8,128)(2,1)}), bf16[2048,1024]{1,0:T(8,128)(2,1)}) %all-gather.5.cloned.1.call-update) | async-done | bytes 4194320 | tf_op jit(solution)/shard_map/all_gather | solution.py:35
  178.1 12.1 %fusion.11 = f32[1024,1024]{1,0:T(8,128)} fusion(bf16[1024,1024]{1,0:T(8,128)(2,1)S(1)} %copy-done.3, bf16[2048,1024]{1,0:T(8,128)(2,1)} %all-gather.5.cloned.1.call-done, bf16[128,8,16,128]{3,2,1,0:T(8,128)(2,1)} %bitcast.107), kind=kOutput, calls=%fused_computation.19 | convolution fusion | flops 6443499520 | bytes 14680064 | tf_op jit(solution)/shard_map/dot_general | solution.py:70
  190.2 13.4 %reduce-scatter.2.cloned.1.call-done = f32[512,1024]{1,0:T(8,128)} async-done(((f32[1024,1024]{1,0:T(8,128)}), f32[512,1024]{1,0:T(8,128)}) %reduce-scatter.2.cloned.1.call-update) | async-done | bytes 2097168 | tf_op jit(solution)/shard_map/reduce_scatter | solution.py:69
  203.5 9.9 %fusion.30 = f32[512,1024]{1,0:T(8,128)S(1)} fusion(f32[512,1024]{1,0:T(8,128)} %reduce-scatter.2.cloned.1.call-done, f32[1024,1024]{1,0:T(8,128)} %copy-done.1, s32[]{:T(128)S(6)} %select_n.63), kind=kOutput, calls=%fused_computation.34 | convolution fusion | flops 6442975232 | bytes 10485764 | tf_op jit(solution)/shard_map/dot_general | solution.py:25
  213.6 6.7 %gather_fusion = f32[512]{0:T(512)} fusion(f32[512,512]{1,0:T(8,128)S(1)} %constant_dynamic-slice_fusion.1, s32[512]{0:T(512)S(1)} %bitcast.104), kind=kCustom, calls=%fused_computation | custom fusion | bytes 8192 | tf_op jit(solution)/shard_map/jit(diagonal)/cond/branch_0_fun/gather | solution.py:79
  (42 shorter events, 4.8 us)
Async XLA Ops:
  7.2 21.7 %all-gather.3.cloned.1.call-start = ((), (), s32[]{:S(2)}) async-start(), calls=%async_computation.2 | async-start | bytes 3145728 | tf_op jit(solution)/shard_map/all_gather | solution.py:21
  16.8 147.3 %all-to-all-start = ((bf16[16,1024,128]{2,1,0:T(8,128)(2,1)}), bf16[16,1024,128]{2,1,0:T(8,128)(2,1)}, u32[]{:S(2)}, u32[]{:S(2)}) async-start(bf16[16,1024,128]{2,1,0:T(8,128)(2,1)} %bitcast.105), calls=%async_computation | async-start | bytes 8388608 | tf_op jit(solution)/shard_map/all_to_all | solution.py:50
  25.2 152.9 %all-gather.5.cloned.1.call-start = ((), (), s32[]{:S(2)}) async-start(), calls=%async_computation.3 | async-start | bytes 6291456 | tf_op jit(solution)/shard_map/all_gather | solution.py:35
  135.0 3.2 %copy-start = (f32[1024,1024]{1,0:T(8,128)S(1)}, f32[1024,1024]{1,0:T(8,128)}, u32[]{:S(2)}) copy-start(f32[1024,1024]{1,0:T(8,128)} %fusion.40) | copy-start | bytes 12582916
  152.5 6.7 %copy-start.5 = (bf16[1024,1024]{1,0:T(8,128)(2,1)S(1)}, bf16[1024,1024]{1,0:T(8,128)(2,1)}, u32[]{:S(2)}) copy-start(bf16[1024,1024]{1,0:T(8,128)(2,1)} %param.6) | copy-start | bytes 6291460
  157.3 2.0 copy-start.1
  159.2 4.6 %copy-start.4 = (s32[16,16]{1,0:T(8,128)S(1)}, s32[16,16]{1,0:T(8,128)}, u32[]{:S(2)}) copy-start(s32[16,16]{1,0:T(8,128)} %param.8) | copy-start | bytes 3076
  163.0 40.5 %reduce-scatter.2.cloned.1.call-start = ((), (), s32[]{:S(2)}) async-start(), calls=%async_computation.4 | async-start | bytes 6291456 | tf_op jit(solution)/shard_map/reduce_scatter | solution.py:69
  169.0 9.1 %copy-start.3 = (bf16[1024,1024]{1,0:T(8,128)(2,1)S(1)}, bf16[1024,1024]{1,0:T(8,128)(2,1)}, u32[]{:S(2)}) copy-start(bf16[1024,1024]{1,0:T(8,128)(2,1)} %fusion.19) | copy-start | bytes 6291460
  213.4 6.9 %copy-start.2 = (f32[512,1024]{1,0:T(8,128)}, f32[512,1024]{1,0:T(8,128)S(1)}, u32[]{:S(2)}) copy-start(f32[512,1024]{1,0:T(8,128)S(1)} %fusion.30) | copy-start | bytes 6291460
Sparse Core Ops, SparseCore 0:
  9.5 13.2 all-gather.2
  163.1 14.9 all-gather.4
  190.3 13.2 reduce-scatter.1
where the time goes:
time: 228 us; the launch traced here: 227 us
  other arithmetic  88.9 us (39%)
  matrix products  53.3 us (23%)
  local copies, waits for them, and re-layouts  41.8 us (18%)
  waiting for transfers between devices  20.2 us (9%)
  between operations  14 us (6%)
  starting transfers between devices  8.51 us (4%)
    another operation x3, other arithmetic, on_device(): lax.linalg.triangular_solve(lower_full, identity, left_side=True, lower=T...  82.9 us
    another operation x24, local copies, waits for them, and re-layouts  23.1 us
    another operation x15, matrix products, on_device(): lax.linalg.triangular_solve(lower_full, identity, left_side=True, lower=T...  22.1 us
    reduce_scatter x1, waiting for transfers between devices, on_device(): lax.psum_scatter(lax.dot_general(wide_mine, carried, (((0,), (0,)), ((),...  13.4 us
    dot_general x1, matrix products, on_device(): lax.dot_general(wide_mine, carried, (((0,), (0,)), ((), ())), preferred_e...  12.1 us
    dot_general x1, matrix products, on_device(): jnp.dot(own_columns.T, inverse, precision=lax.Precision.HIGHEST)  9.9 us
    all_to_all x1, starting transfers between devices, on_device(): lax.all_to_all(outgoing, 'front', split_axis=0, concat_axis=0, tiled=True)  8.39 us
    gather x1, local copies, waits for them, and re-layouts, on_device(): variances = jnp.diagonal(diagonal_block)  6.73 us
  transfers between devices with their start and end apart: 4, of which 2 were waited for; matrix products, arithmetic and copies ran while one was open for 68% of the time, Pallas kernels for 0%

commit v1 on v0

v1 whole, which is shorter than its diff:
```python
import functools

import jax
import jax.numpy as jnp
from jax import lax
from jax.experimental import pallas as pl
from jax.experimental.pallas import tpu as pltpu
from jax.sharding import PartitionSpec as P

BF = jnp.bfloat16
F32 = jnp.float32
DIAG = 128


def mm(a, b):
    return jnp.dot(a, b, preferred_element_type=F32)


def split(x):
    hi = x.astype(BF)
    return hi, (x - hi.astype(F32)).astype(BF)


def invert(lmat, xh, xl, xd):
    n = lmat.shape[0]
    blocks = n // DIAG
    row = lax.broadcasted_iota(jnp.int32, (DIAG, DIAG), 0)
    col = lax.broadcasted_iota(jnp.int32, (DIAG, DIAG), 1)
    eye = row == col
    xh[...] = jnp.zeros_like(xh)
    xl[...] = jnp.zeros_like(xl)
    for b in range(blocks):
        span = pl.ds(b * DIAG, DIAG)
        block = lmat[span, span].astype(F32)
        xd[b] = jnp.where(eye, 1.0 / jnp.where(eye, block, 1.0), 0.0)

    def level(step, carry):
        mask = (
            ((row >> (step + 1)) == (col >> (step + 1)))
            & (((row >> step) & 1) == 1)
            & (((col >> step) & 1) == 0)
        )
        for b in range(blocks):
            span = pl.ds(b * DIAG, DIAG)
            x = xd[b]
            hi, lo = split(x)
            below = jnp.where(mask, lmat[span, span].astype(F32), 0.0).astype(BF)
            y = mm(below, jnp.concatenate([hi, lo], axis=1))
            yhi, ylo = split(y[:, :DIAG] + y[:, DIAG:])
            z = mm(jnp.concatenate([hi, lo], axis=0), jnp.concatenate([yhi, ylo], axis=1))
            z = (z[:DIAG, :DIAG] + z[:DIAG, DIAG:]) + (z[DIAG:, :DIAG] + z[DIAG:, DIAG:])
            xd[b] = x - z
        return carry

    levels = DIAG.bit_length() - 1
    lax.fori_loop(0, levels, level, 0)
    for b in range(blocks):
        span = pl.ds(b * DIAG, DIAG)
        xh[span, span], xl[span, span] = split(xd[b])
    size = DIAG
    while size < n:
        for start in range(0, n, 2 * size):
            top, low = pl.ds(start, size), pl.ds(start + size, size)
            below = lmat[low, top]
            thi, tlo = split(mm(below, xh[top, top]) + mm(below, xl[top, top]))
            z = mm(xh[low, low], thi) + (mm(xh[low, low], tlo) + mm(xl[low, low], thi))
            xh[low, top], xl[low, top] = split(-z)
        size *= 2


def first_kernel(sep_ref, sep_other, coup_ref, coup_other, live_ref, inv_ref, wide_ref, lmat, xl, xd):
    me = lax.axis_index("panel")
    half = sep_ref.shape[0]
    lmat[pl.ds(pl.multiple_of(me * half, half), half), :] = sep_ref[...]
    lmat[pl.ds(pl.multiple_of((1 - me) * half, half), half), :] = sep_other[...]
    invert(lmat, inv_ref, xl, xd)
    rows = coup_ref.shape[0]
    chunk = min(512, rows)
    columns = pl.ds(pl.multiple_of(me * half, half), half)

    @pl.loop(0, rows // chunk)
    def _(i):
        for source, base in ((coup_ref, 0), (coup_other, rows)):
            take = pl.ds(pl.multiple_of(i * chunk, chunk), chunk)
            put = pl.ds(pl.multiple_of(base + i * chunk, chunk), chunk)
            w = mm(source[take, :], inv_ref[:, columns])
            wide_ref[put, :] = jnp.where(live_ref[put, :] > 0, w, 0.0).astype(BF)


def last_kernel(where_ref, wide_ref, wide_other, inv_ref, pool_ref, out_ref, var_ref, sigma, sem):
    me = lax.axis_index("panel")
    rows, half = wide_ref.shape
    edge = pool_ref.shape[1]
    width = inv_ref.shape[1]
    strips = where_ref.shape[0]
    strip_rows = rows * rows // (strips * edge)
    across = rows // edge

    def tile_copy(k):
        source = pl.ds(pl.multiple_of(where_ref[k] * strip_rows, strip_rows), strip_rows)
        down = pl.multiple_of((k // across) * strip_rows, strip_rows)
        over = pl.multiple_of((k % across) * edge, edge)
        return pltpu.make_async_copy(
            pool_ref.at[source, :], sigma.at[pl.ds(down, strip_rows), pl.ds(over, edge)], sem
        )

    @pl.loop(0, strips)
    def _(k):
        tile_copy(k).start()

    mine = pl.ds(pl.multiple_of(me * half, half), half)
    other = pl.ds(pl.multiple_of((1 - me) * half, half), half)
    contract = (((0,), (0,)), ((), ()))

    def tmm(a, b):
        return lax.dot_general(a, b, contract, preferred_element_type=F32)

    out_ref[...] = tmm(inv_ref[:, mine], inv_ref[...])
    pltpu.make_async_copy(pool_ref.at[pl.ds(0, rows * rows // edge), :], pool_ref.at[pl.ds(0, rows * rows // edge), :], sem).wait()
    chunk = rows // 4

    @pl.loop(0, 4)
    def _(i):
        take = pl.ds(pl.multiple_of(i * chunk, chunk), chunk)
        swapped = pl.ds(pl.multiple_of(((i + 2) % 4) * chunk, chunk), chunk)
        carried = mm(sigma[take, :], wide_ref[...]).astype(BF)
        out_ref[:, mine] += tmm(carried, wide_ref[take, :])
        out_ref[:, other] += tmm(carried, wide_other[swapped, :])

    block = out_ref[:, mine]
    row = lax.broadcasted_iota(jnp.int32, (half, half), 0)
    col = lax.broadcasted_iota(jnp.int32, (half, half), 1)
    var_ref[...] = jnp.sum(jnp.where(row == col, block, 0.0), axis=0, keepdims=True)


def on_device(sep_factor, coup_factor, coup_list, slot_tiles, anc_tiles):
    panels = lax.axis_size("panel")
    groups = lax.axis_size("front")
    me = lax.axis_index("panel")
    my_group = lax.axis_index("front")
    half, width = sep_factor.shape
    edge = anc_tiles.shape[1]
    slots = slot_tiles.shape[1]
    strip_rows = anc_tiles.shape[0] // slots
    strip_count = edge // strip_rows
    list_width = coup_list.shape[1]
    row_blocks = list_width // panels
    rows = list_width * edge
    swap = [(0, 1), (1, 0)]
    vmem = pl.BlockSpec(memory_space=pltpu.VMEM)

    part = anc_tiles.shape[0] // panels
    pool = lax.all_gather(
        lax.dynamic_slice_in_dim(anc_tiles, me * part, part), ("front", "panel"), axis=0, tiled=True
    )
    sep_other = lax.ppermute(sep_factor, "panel", swap)
    coup_other = lax.ppermute(coup_factor, "panel", swap)

    own_list = coup_list[my_group]
    own_list = jnp.where(me == 0, own_list, jnp.roll(own_list, -row_blocks))
    live = jnp.repeat((own_list >= 0).astype(F32), edge)[:, None]
    blocks = jnp.maximum(own_list, 0)
    wanted = (
        blocks[:, None, None] * groups
        + jnp.arange(strip_count, dtype=jnp.int32)[None, :, None]
        + blocks[None, None, :] * strip_count
    ).reshape(-1)
    flat = slot_tiles.reshape(-1)
    place = jnp.sum(
        jnp.where(
            wanted[:, None] == flat[None, :], jnp.arange(flat.shape[0], dtype=jnp.int32)[None, :], 0
        ),
        axis=1,
    )

    inverse, wide = pl.pallas_call(
        first_kernel,
        out_shape=(
            jax.ShapeDtypeStruct((width, width), BF),
            jax.ShapeDtypeStruct((rows, half), BF),
        ),
        in_specs=[vmem] * 5,
        out_specs=[vmem] * 2,
        scratch_shapes=[
            pltpu.VMEM((width, width), BF),
            pltpu.VMEM((width, width), BF),
            pltpu.VMEM((width // DIAG, DIAG, DIAG), F32),
        ],
        compiler_params=pltpu.CompilerParams(vmem_limit_bytes=48 << 20),
        cost_estimate=pl.CostEstimate(flops=20 * 10**9, bytes_accessed=12 << 20, transcendentals=0),
    )(sep_factor, sep_other, coup_factor, coup_other, live)
    wide_other = lax.ppermute(wide, "panel", swap)
    selected, variances = pl.pallas_call(
        last_kernel,
        out_shape=(
            jax.ShapeDtypeStruct((half, width), F32),
            jax.ShapeDtypeStruct((1, half), F32),
        ),
        in_specs=[pl.BlockSpec(memory_space=pltpu.SMEM), vmem, vmem, vmem, pl.BlockSpec(memory_space=pl.ANY)],
        out_specs=[vmem] * 2,
        scratch_shapes=[pltpu.VMEM((rows, rows), BF), pltpu.SemaphoreType.DMA],
        compiler_params=pltpu.CompilerParams(vmem_limit_bytes=48 << 20),
    )(place, wide, wide_other, inverse, pool)
    return selected, variances.reshape(half)


def solution(mesh):
    placed = (P(("front", "panel"), None), P(("front", "panel"), None), P(), P(), P("front", None))
    return jax.shard_map(
        on_device,
        mesh=mesh,
        in_specs=placed,
        out_specs=(P(("front", "panel"), None), P(("front", "panel"))),
        check_vma=False,
    )
```

time: 228 us -> 122 us (0.54); the launches traced: 227 us -> 124 us
  other arithmetic: 88.9 us -> 1.06 us
  matrix products: 53.3 us -> 0 us
  Pallas kernels: 0 us -> 41.6 us
  waiting for transfers between devices: 20.2 us -> 59 us
  local copies, waits for them, and re-layouts: 41.8 us -> 7.25 us
  starting transfers between devices: 8.51 us -> 1.07 us
    another operation x3 -> x0, other arithmetic: 82.9 us -> none  [on_device(): lax.linalg.triangular_solve(lower_full, identity, left_side=True, lower=T...]
    all_gather x2 -> x1, waiting for transfers between devices: 6.17 us -> 52 us  [on_device(): lax.all_gather(lax.dynamic_slice_in_dim(anc_tiles, me * part, part), ('fr...]
    pallas_call x0 -> x2, Pallas kernels: none -> 41.6 us  [the longest x1 25 us: on_device(): pl.pallas_call(last_kernel, out_shape=(jax.ShapeDtypeStruct((half, width)...]
    dot_general x6 -> x0, matrix products: 31.2 us -> none  [the longest x1 12.1 us: on_device(): lax.dot_general(wide_mine, carried, (((0,), (0,)), ((), ())), preferred_e...]
    another operation x25 -> x1, local copies, waits for them, and re-layouts: 23.1 us -> 0.37 us  [on_device(): live = jnp.repeat((own_list >= 0).astype(F32), edge)[:, None]]
    another operation x15 -> x0, matrix products: 22.1 us -> none  [on_device(): lax.linalg.triangular_solve(lower_full, identity, left_side=True, lower=T...]
    reduce_scatter x1 -> x0, waiting for transfers between devices: 13.4 us -> none  [on_device(): lax.psum_scatter(lax.dot_general(wide_mine, carried, (((0,), (0,)), ((),...]
    all_to_all x1 -> x0, starting transfers between devices: 8.39 us -> none  [on_device(): lax.all_to_all(outgoing, 'front', split_axis=0, concat_axis=0, tiled=True)]
  transfers between devices with their start and end apart: 4 -> 4, of which waited for: 2 -> 3; matrix products, arithmetic and copies ran while one was open for 68% -> 2% of each run, Pallas kernels for 0% -> 13%
where the time goes in v1:
time: 122 us; the launch traced here: 124 us
  waiting for transfers between devices  59 us (48%)
  Pallas kernels  41.6 us (34%)
  between operations  14.1 us (12%)
  local copies, waits for them, and re-layouts  7.25 us (6%)
    all_gather x1, waiting for transfers between devices, on_device(): lax.all_gather(lax.dynamic_slice_in_dim(anc_tiles, me * part, part), ('fr...  52 us
    pallas_call x1, Pallas kernels, on_device(): pl.pallas_call(last_kernel, out_shape=(jax.ShapeDtypeStruct((half, width)...  25 us
    pallas_call x1, Pallas kernels, on_device(): pl.pallas_call(first_kernel, out_shape=(jax.ShapeDtypeStruct((width, widt...  16.7 us
    unnamed x10, local copies, waits for them, and re-layouts  5.17 us
    ppermute x1, waiting for transfers between devices, on_device(): wide_other = lax.ppermute(wide, 'panel', swap)  3.53 us
    ppermute x1, waiting for transfers between devices, on_device(): sep_other = lax.ppermute(sep_factor, 'panel', swap)  3.44 us
  transfers between devices with their start and end apart: 4, of which 3 were waited for; matrix products, arithmetic and copies ran while one was open for 2% of the time, Pallas kernels for 13%

profile of v1, /device:TPU:0, one launch (start us, length us, event | category | flops | bytes accessed | tf_op | source)
XLA Modules:
  0.0 124.1 jit_solution(7863618648373663129)
XLA Ops:
  7.2 0.0 copy-start
  7.2 0.0 all-gather.2.cloned.1.call-start
  7.2 1.0 copy-done
  8.2 0.7 constant_dynamic-slice_fusion
  8.9 0.0 all-gather.2.cloned.1.call-update
  9.0 0.6 collective-permute-start.1
  9.5 0.1 collective-permute-start
  9.6 0.7 constant_dynamic-slice_fusion.1
  10.3 0.1 slice_bitcast_fusion.1
  10.4 0.8 compare_convert_fusion
  11.1 0.1 broadcast_in_dim.20
  11.2 0.0 copy-start.4
  11.2 0.4 copy.8.live_ref
  11.6 3.4 %collective-permute-done.sep_other = bf16[512,1024]{1,0:T(8,128)(2,1)S(1)} collective-permute-done((bf16[512,1024]{1,0:T(8,128)(2,1)}, bf16[512,1024]{1,0:T(8,128)(2,1)S(1)}, u32[]{:S(2)}, u32[]{:S(2)}) %collective-permute-start) | collective-permute-done | bytes 1048608 | tf_op jit(solution)/shard_map/ppermute | solution.py:156
  15.0 0.0 collective-permute-done.1.coup_other
  15.0 0.0 copy-start.3
  15.0 1.2 copy-done.3
  16.2 16.7 %shard_map.68 = (bf16[1024,1024]{1,0:T(8,128)(2,1)S(1)}, bf16[2048,512]{1,0:T(8,128)(2,1)}) custom-call(bf16[512,1024]{1,0:T(8,128)(2,1)S(1)} %copy-done.3, bf16[512,1024]{1,0:T(8,128)(2,1)S(1)} %collective-permute-done.sep_other, bf16[1024,1024]{1,0:T(8,128)(2,1)} %coup_ref.1, bf16[1024,1024]{1,0:T(8,128)(2,1)} %collective-permute-done.1.coup_other, ...), custom_call_target="tpu_custom_call" | custom-call | flops 20000000000 | bytes 12582912 | tf_op jit(solution)/shard_map/pallas_call | solution.py:176
  32.9 0.0 copy-start.1
  32.9 1.4 %copy-done.1 = bf16[1024,1024]{1,0:T(8,128)(2,1)} copy-done((bf16[1024,1024]{1,0:T(8,128)(2,1)}, bf16[1024,1024]{1,0:T(8,128)(2,1)S(1)}, u32[]{:S(2)}) %copy-start.1) | copy-done | bytes 2097176
  34.3 0.4 collective-permute-start.2
  34.7 0.0 copy-done.4
  34.7 0.1 eq.20
  34.7 0.1 add_reduce_fusion
  34.9 0.1 add.32
  34.9 0.2 select_reduce_fusion.where_ref
  35.1 3.5 %collective-permute-done.2.wide_other = bf16[2048,512]{1,0:T(8,128)(2,1)S(1)} collective-permute-done((bf16[2048,512]{1,0:T(8,128)(2,1)}, bf16[2048,512]{1,0:T(8,128)(2,1)S(1)}, u32[]{:S(2)}, u32[]{:S(2)}) %collective-permute-start.2) | collective-permute-done | bytes 2097184 | tf_op jit(solution)/shard_map/ppermute | solution.py:192
  38.7 52.0 %all-gather.2.cloned.1.call-done.pool_ref = bf16[32768,128]{1,0:T(8,128)(2,1)} async-done(((bf16[1024,128]{1,0:T(8,128)(2,1)}), bf16[32768,128]{1,0:T(8,128)(2,1)}) %all-gather.2.cloned.1.call-update) | async-done | bytes 8388624 | tf_op jit(solution)/shard_map/all_gather | solution.py:153
  90.7 0.0 copy-start.2
  90.7 1.6 %copy-done.2 = bf16[2048,512]{1,0:T(8,128)(2,1)S(1)} copy-done((bf16[2048,512]{1,0:T(8,128)(2,1)S(1)}, bf16[2048,512]{1,0:T(8,128)(2,1)}, u32[]{:S(2)}) %copy-start.2) | copy-done | bytes 2097176
  92.3 25.0 %shard_map.69 = (f32[512,1024]{1,0:T(8,128)}, f32[1,512]{1,0:T(1,128)}) custom-call(s32[256]{0:T(256)S(1)} %select_reduce_fusion.where_ref, bf16[2048,512]{1,0:T(8,128)(2,1)S(1)} %copy-done.2, bf16[2048,512]{1,0:T(8,128)(2,1)S(1)} %collective-permute-done.2.wide_other, bf16[1024,1024]{1,0:T(8,128)(2,1)} %copy-done.1, ...), custom_call_target="tpu_custom_call" | custom-call | tf_op jit(solution)/shard_map/pallas_call | solution.py:193
  (1 shorter events, 0.0 us)
Async XLA Ops:
  7.2 1.0 copy-start
  7.2 83.5 %all-gather.2.cloned.1.call-start = ((), (), s32[]{:S(2)}) async-start(), calls=%async_computation | async-start | bytes 8650752 | tf_op jit(solution)/shard_map/all_gather | solution.py:153
  9.0 6.1 %collective-permute-start.1 = (bf16[1024,1024]{1,0:T(8,128)(2,1)}, bf16[1024,1024]{1,0:T(8,128)(2,1)}, u32[]{:S(2)}, u32[]{:S(2)}) collective-permute-start(bf16[1024,1024]{1,0:T(8,128)(2,1)} %coup_ref.1), channel_id=1, source_target_pairs={{0,1},{1,0},{2,3},{3,2},{4,5},{5,4},{6,7},{7,6},{8,9},{9,8},{10,11... | collective-permute-start | bytes 6291464 | tf_op jit(solution)/shard_map/ppermute | solution.py:157
  9.5 5.5 %collective-permute-start = (bf16[512,1024]{1,0:T(8,128)(2,1)}, bf16[512,1024]{1,0:T(8,128)(2,1)S(1)}, u32[]{:S(2)}, u32[]{:S(2)}) collective-permute-start(bf16[512,1024]{1,0:T(8,128)(2,1)} %sep_ref.1), channel_id=1, source_target_pairs={{0,1},{1,0},{2,3},{3,2},{4,5},{5,4},{6,7},{7,6},{8,9},{9,8},{10,11... | collective-permute-start | bytes 3145736 | tf_op jit(solution)/shard_map/ppermute | solution.py:156
  11.2 23.5 %copy-start.4 = (s32[16,16]{1,0:T(8,128)S(1)}, s32[16,16]{1,0:T(8,128)}, u32[]{:S(2)}) copy-start(s32[16,16]{1,0:T(8,128)} %param.8) | copy-start | bytes 3076
  15.0 1.2 copy-start.3
  32.9 1.4 %copy-start.1 = (bf16[1024,1024]{1,0:T(8,128)(2,1)}, bf16[1024,1024]{1,0:T(8,128)(2,1)S(1)}, u32[]{:S(2)}) copy-start(bf16[1024,1024]{1,0:T(8,128)(2,1)S(1)} %get-tuple-element.7.inv_ref) | copy-start | bytes 6291460
  34.3 4.4 %collective-permute-start.2 = (bf16[2048,512]{1,0:T(8,128)(2,1)}, bf16[2048,512]{1,0:T(8,128)(2,1)S(1)}, u32[]{:S(2)}, u32[]{:S(2)}) collective-permute-start(bf16[2048,512]{1,0:T(8,128)(2,1)} %get-tuple-element.6.wide_ref), channel_id=1, source_target_pairs={{0,1},{1,0},{2,3},{3,2},{4,5},{5,4},{6,7},{7,6},{8,9},{9,8},{10,11... | collective-permute-start | bytes 6291464 | tf_op jit(solution)/shard_map/ppermute | solution.py:192
  90.7 1.6 %copy-start.2 = (bf16[2048,512]{1,0:T(8,128)(2,1)S(1)}, bf16[2048,512]{1,0:T(8,128)(2,1)}, u32[]{:S(2)}) copy-start(bf16[2048,512]{1,0:T(8,128)(2,1)} %get-tuple-element.6.wide_ref) | copy-start | bytes 6291460
Sparse Core Ops, SparseCore 0:
  10.8 79.7 all-gather.1

commit v2 on v1

v2 whole, which is shorter than its diff:
```python
import functools

import jax
import jax.numpy as jnp
from jax import lax
from jax.experimental import pallas as pl
from jax.experimental.pallas import tpu as pltpu
from jax.sharding import PartitionSpec as P

BF = jnp.bfloat16
F32 = jnp.float32
DIAG = 128
MESH = pl.DeviceIdType.MESH


def mm(a, b):
    return jnp.dot(a, b, preferred_element_type=F32)


def split(x):
    hi = x.astype(BF)
    return hi, (x - hi.astype(F32)).astype(BF)


def flip(index, mask):
    bit = 1
    while bit <= mask:
        if mask & bit:
            index = index + bit * (1 - 2 * ((index // bit) % 2))
        bit *= 2
    return index


def first_kernel(
    depth,
    sep_ref,
    coup_ref,
    live_ref,
    anc_ref,
    inv_ref,
    wide_ref,
    wide_other,
    square_ref,
    pool_ref,
    lmat,
    sep_other,
    coup_other,
    xl,
    xd,
    panel_send,
    panel_recv,
    z_recv,
    x_recv,
    y_recv,
    first_recv,
    second_recv,
    share_recv,
    out_send,
    local_sem,
):
    me = lax.axis_index("panel")
    group = lax.axis_index("front")
    layer, spot = group // 4, group % 4
    half, n = sep_ref.shape[0], sep_ref.shape[1]
    slab = anc_ref.shape[0]
    part = slab // 2
    partner = (group, 1 - me)
    beside = (layer * 4 + flip(spot, 1), me)
    behind = (layer * 4 + flip(spot, 2), me)
    peers = [(flip(layer, k) * 4 + spot, me) for k in range(1, depth)]

    barrier = pltpu.get_barrier_semaphore()
    for device in [partner, beside, behind] + peers:
        pl.semaphore_signal(barrier, inc=1, device_id=device, device_id_type=MESH)
    pl.semaphore_wait(barrier, 2 + depth)

    def remote(source, target, send, recv, device):
        return pltpu.make_async_remote_copy(
            src_ref=source, dst_ref=target, send_sem=send, recv_sem=recv, device_id=device, device_id_type=MESH
        )

    def place(k, mask, low=0, size=part):
        owner = flip(layer, k) * 4 + flip(spot, mask)
        start = pl.multiple_of(owner * slab + me * part + low, part // 2)
        return pool_ref.at[pl.ds(start, size), :]

    def push(source, target, recv, device):
        remote(source, target, out_send, recv, device).start()

    def arrived(target, recv):
        remote(target, target, out_send, recv, partner).wait_recv()

    own = anc_ref.at[pl.ds(pl.multiple_of(me * part, part), part), :]

    def open_block(k):
        source = own if k == 0 else place(k, 0)
        if k > 0:
            arrived(source, z_recv.at[k])
        push(source, place(k, 0), x_recv.at[k], beside)
        push(source, place(k, 0), y_recv.at[k], behind)
        if k > 0:
            push(source, source, share_recv, partner)

    def relay(k):
        piece = part // 2
        arrived(place(k, 1), x_recv.at[k])
        push(place(k, 1, piece, piece), place(k, 1, piece, piece), second_recv.at[k], behind)
        arrived(place(k, 2), y_recv.at[k])
        push(place(k, 2, 0, piece), place(k, 2, 0, piece), first_recv.at[k], beside)
        push(place(k, 1), place(k, 1), share_recv, partner)
        push(place(k, 2), place(k, 2), share_recv, partner)

    def finish(k):
        piece = part // 2
        arrived(place(k, 3, 0, piece), first_recv.at[k])
        arrived(place(k, 3, piece, piece), second_recv.at[k])
        push(place(k, 3), place(k, 3), share_recv, partner)

    def stage(k):
        if k < depth:
            open_block(k)
        if 1 <= k <= depth:
            relay(k - 1)
        if 2 <= k <= depth + 1:
            finish(k - 2)

    sep_copy = remote(sep_ref, sep_other, panel_send.at[0], panel_recv.at[0], partner)
    coup_copy = remote(coup_ref, coup_other, panel_send.at[1], panel_recv.at[1], partner)
    wide_copy = remote(wide_ref, wide_other, panel_send.at[2], panel_recv.at[2], partner)
    sep_copy.start()
    for k in range(1, depth):
        push(own, place(0, 0), z_recv.at[k], peers[k - 1])
        if k == 1:
            stage(0)
    coup_copy.start()
    keep = pltpu.make_async_copy(
        anc_ref, pool_ref.at[pl.ds(pl.multiple_of(group * slab, slab), slab), :], local_sem
    )
    keep.start()

    lmat[pl.ds(pl.multiple_of(me * half, half), half), :] = sep_ref[...]
    inv_ref[...] = jnp.zeros_like(inv_ref)
    xl[...] = jnp.zeros_like(xl)
    sep_copy.wait_recv()
    lmat[pl.ds(pl.multiple_of((1 - me) * half, half), half), :] = sep_other[...]

    blocks = n // DIAG
    row = lax.broadcasted_iota(jnp.int32, (DIAG, DIAG), 0)
    col = lax.broadcasted_iota(jnp.int32, (DIAG, DIAG), 1)
    eye = row == col
    for b in range(blocks):
        span = pl.ds(b * DIAG, DIAG)
        block = lmat[span, span].astype(F32)
        xd[b] = jnp.where(eye, 1.0 / jnp.where(eye, block, 1.0), 0.0)

    def level(step, carry):
        mask = (
            ((row >> (step + 1)) == (col >> (step + 1)))
            & (((row >> step) & 1) == 1)
            & (((col >> step) & 1) == 0)
        )
        for b in range(blocks):
            span = pl.ds(b * DIAG, DIAG)
            x = xd[b]
            hi, lo = split(x)
            below = jnp.where(mask, lmat[span, span].astype(F32), 0.0).astype(BF)
            y = mm(below, jnp.concatenate([hi, lo], axis=1))
            yhi, ylo = split(y[:, :DIAG] + y[:, DIAG:])
            t = mm(jnp.concatenate([hi, lo], axis=0), jnp.concatenate([yhi, ylo], axis=1))
            t = (t[:DIAG, :DIAG] + t[:DIAG, DIAG:]) + (t[DIAG:, :DIAG] + t[DIAG:, DIAG:])
            xd[b] = x - t
        return carry

    levels = DIAG.bit_length() - 1
    lax.fori_loop(0, levels // 2, level, 0)
    stage(1)
    lax.fori_loop(levels // 2, levels, level, 0)
    for b in range(blocks):
        span = pl.ds(b * DIAG, DIAG)
        inv_ref[span, span], xl[span, span] = split(xd[b])
    size = DIAG
    while size < n:
        for start in range(0, n, 2 * size):
            top, low = pl.ds(start, size), pl.ds(start + size, size)
            below = lmat[low, top]
            thi, tlo = split(mm(below, inv_ref[top, top]) + mm(below, xl[top, top]))
            t = mm(inv_ref[low, low], thi) + (mm(inv_ref[low, low], tlo) + mm(xl[low, low], thi))
            inv_ref[low, top], xl[low, top] = split(-t)
        size *= 2
    stage(2)

    rows = coup_ref.shape[0]
    chunk = min(512, rows)
    columns = pl.ds(pl.multiple_of(me * half, half), half)
    coup_copy.wait_recv()

    @pl.loop(0, rows // chunk)
    def _(i):
        for source, base in ((coup_ref, 0), (coup_other, rows)):
            take = pl.ds(pl.multiple_of(i * chunk, chunk), chunk)
            put = pl.ds(pl.multiple_of(base + i * chunk, chunk), chunk)
            w = mm(source[take, :], inv_ref[:, columns])
            wide_ref[put, :] = jnp.where(live_ref[put, :] > 0, w, 0.0).astype(BF)

    stage(3)
    wide_copy.start()

    @pl.loop(0, n // 256)
    def _(i):
        take = pl.ds(pl.multiple_of(i * 256, 256), 256)
        square_ref[:, take] = lax.dot_general(
            inv_ref[:, columns], inv_ref[:, take], (((0,), (0,)), ((), ())), preferred_element_type=F32
        )

    for k in range(4, depth + 2):
        stage(k)

    total = 4 * depth - 1
    shared = pool_ref.at[pl.ds(0, total * part), :]
    remote(shared, shared, out_send, share_recv, partner).wait_recv()
    sent = pool_ref.at[pl.ds(0, (2 * total) * part), :]
    remote(sent, sent, out_send, share_recv, partner).wait_send()
    keep.wait()
    sep_copy.wait_send()
    coup_copy.wait_send()
    wide_copy.wait()


def last_kernel(where_ref, wide_ref, wide_other, square_ref, pool_ref, out_ref, var_ref, sigma, sem):
    me = lax.axis_index("panel")
    rows, half = wide_ref.shape
    edge = pool_ref.shape[1]
    strips = where_ref.shape[0]
    strip_rows = rows * rows // (strips * edge)
    across = rows // edge
    chunks = sem.shape[0]
    chunk = rows // chunks

    @pl.loop(0, strips)
    def _(k):
        source = pl.ds(pl.multiple_of(where_ref[k] * strip_rows, strip_rows), strip_rows)
        down = pl.multiple_of((k // across) * strip_rows, strip_rows)
        over = pl.multiple_of((k % across) * edge, edge)
        pltpu.make_async_copy(
            pool_ref.at[source, :],
            sigma.at[pl.ds(down, strip_rows), pl.ds(over, edge)],
            sem.at[k // (strips // chunks)],
        ).start()

    mine = pl.ds(pl.multiple_of(me * half, half), half)
    other = pl.ds(pl.multiple_of((1 - me) * half, half), half)

    def tmm(a, b):
        return lax.dot_general(a, b, (((0,), (0,)), ((), ())), preferred_element_type=F32)

    out_ref[...] = square_ref[...]

    @pl.loop(0, chunks)
    def _(i):
        take = pl.ds(pl.multiple_of(i * chunk, chunk), chunk)
        turned = ((i + chunks // 2) % chunks) * chunk
        swapped = pl.ds(pl.multiple_of(turned, chunk), chunk)
        pltpu.make_async_copy(sigma.at[take, :], sigma.at[take, :], sem.at[i]).wait()
        carried = mm(sigma[take, :], wide_ref[...]).astype(BF)
        out_ref[:, mine] += tmm(carried, wide_ref[take, :])
        out_ref[:, other] += tmm(carried, wide_other[swapped, :])

    block = out_ref[:, mine]
    row = lax.broadcasted_iota(jnp.int32, (half, half), 0)
    col = lax.broadcasted_iota(jnp.int32, (half, half), 1)
    var_ref[...] = jnp.sum(jnp.where(row == col, block, 0.0), axis=0, keepdims=True)


def on_device(sep_factor, coup_factor, coup_list, slot_tiles, anc_tiles):
    panels = lax.axis_size("panel")
    groups = lax.axis_size("front")
    me = lax.axis_index("panel")
    my_group = lax.axis_index("front")
    half, width = sep_factor.shape
    edge = anc_tiles.shape[1]
    slots = slot_tiles.shape[1]
    strip_rows = anc_tiles.shape[0] // slots
    strip_count = edge // strip_rows
    list_width = coup_list.shape[1]
    row_blocks = list_width // panels
    rows = list_width * edge
    vmem = pl.BlockSpec(memory_space=pltpu.VMEM)
    hbm = pl.BlockSpec(memory_space=pl.ANY)

    own_list = coup_list[my_group]
    own_list = jnp.where(me == 0, own_list, jnp.roll(own_list, -row_blocks))
    live = jnp.repeat((own_list >= 0).astype(F32), edge)[:, None]
    blocks = jnp.maximum(own_list, 0)
    wanted = (
        blocks[:, None, None] * groups
        + jnp.arange(strip_count, dtype=jnp.int32)[None, :, None]
        + blocks[None, None, :] * strip_count
    ).reshape(-1)
    flat = slot_tiles.reshape(-1)
    place = jnp.sum(
        jnp.where(
            wanted[:, None] == flat[None, :], jnp.arange(flat.shape[0], dtype=jnp.int32)[None, :], 0
        ),
        axis=1,
    )

    depth = groups // 4
    dma = pltpu.SemaphoreType.DMA
    _, wide, wide_other, square, pool = pl.pallas_call(
        functools.partial(first_kernel, depth),
        out_shape=(
            jax.ShapeDtypeStruct((width, width), BF),
            jax.ShapeDtypeStruct((rows, half), BF),
            jax.ShapeDtypeStruct((rows, half), BF),
            jax.ShapeDtypeStruct((half, width), F32),
            jax.ShapeDtypeStruct((groups * anc_tiles.shape[0], edge), BF),
        ),
        in_specs=[vmem] * 3 + [hbm],
        out_specs=[vmem] * 4 + [hbm],
        scratch_shapes=[
            pltpu.VMEM((width, width), BF),
            pltpu.VMEM((half, width), BF),
            pltpu.VMEM((rows // panels, width), BF),
            pltpu.VMEM((width, width), BF),
            pltpu.VMEM((width // DIAG, DIAG, DIAG), F32),
            dma((3,)),
            dma((3,)),
            dma((depth,)),
            dma((depth,)),
            dma((depth,)),
            dma((depth,)),
            dma((depth,)),
            dma,
            dma,
            dma,
        ],
        compiler_params=pltpu.CompilerParams(
            vmem_limit_bytes=48 << 20, collective_id=0, has_side_effects=True
        ),
    )(sep_factor, coup_factor, live, anc_tiles)
    selected, variances = pl.pallas_call(
        last_kernel,
        out_shape=(
            jax.ShapeDtypeStruct((half, width), F32),
            jax.ShapeDtypeStruct((1, half), F32),
        ),
        in_specs=[pl.BlockSpec(memory_space=pltpu.SMEM), vmem, vmem, vmem, hbm],
        out_specs=[vmem] * 2,
        scratch_shapes=[pltpu.VMEM((rows, rows), BF), dma((4,))],
        compiler_params=pltpu.CompilerParams(vmem_limit_bytes=48 << 20),
    )(place, wide, wide_other, square, pool)
    return selected, variances.reshape(half)


def solution(mesh):
    placed = (P(("front", "panel"), None), P(("front", "panel"), None), P(), P(), P("front", None))
    return jax.shard_map(
        on_device,
        mesh=mesh,
        in_specs=placed,
        out_specs=(P(("front", "panel"), None), P(("front", "panel"))),
        check_vma=False,
    )
```

time: 122 us -> 80.7 us (0.66); the launches traced: 124 us -> 79.4 us
  waiting for transfers between devices: 59 us -> 0 us
  Pallas kernels: 41.6 us -> 70.1 us
  between operations: 14.1 us -> 0.68 us
    all_gather x1 -> x0, waiting for transfers between devices: 52 us -> none  [on_device(): lax.all_gather(lax.dynamic_slice_in_dim(anc_tiles, me * part, part), ('fr...]
    pallas_call x1, Pallas kernels: 16.7 us -> 54.7 us  [on_device(): pl.pallas_call(functools.partial(first_kernel, depth), out_shape=(jax.Sha...]
    pallas_call x1, Pallas kernels: 25 us -> 15.4 us  [on_device(): pl.pallas_call(last_kernel, out_shape=(jax.ShapeDtypeStruct((half, width)...]
    ppermute x3 -> x0, waiting for transfers between devices: 6.97 us -> none  [the longest x1 3.53 us: on_device(): wide_other = lax.ppermute(wide, 'panel', swap)]
    unnamed x10 -> x8, local copies, waits for them, and re-layouts: 5.17 us -> 5.44 us
  transfers between devices with their start and end apart: 4 -> 0, of which waited for: 3 -> 0; matrix products, arithmetic and copies ran while one was open for 2% -> 0% of each run, Pallas kernels for 13% -> 0%
where the time goes in v2:
time: 80.7 us; the launch traced here: 79.4 us
  Pallas kernels  70.1 us (87%)
  local copies, waits for them, and re-layouts  7.51 us (9%)
  other arithmetic  1.05 us (1%)
    pallas_call x1, Pallas kernels, on_device(): pl.pallas_call(functools.partial(first_kernel, depth), out_shape=(jax.Sha...  54.7 us
    pallas_call x1, Pallas kernels, on_device(): pl.pallas_call(last_kernel, out_shape=(jax.ShapeDtypeStruct((half, width)...  15.4 us
    unnamed x8, local copies, waits for them, and re-layouts  5.44 us

profile of v2, /device:TPU:0, one launch (start us, length us, event | category | flops | bytes accessed | tf_op | source)
XLA Modules:
  0.0 79.4 jit_solution(3640045920656058057)
XLA Ops:
  0.6 0.7 constant_dynamic-slice_fusion
  1.3 0.1 slice_bitcast_fusion.1
  1.4 0.8 compare_convert_fusion
  2.2 0.8 eq.20
  3.0 0.1 add_reduce_fusion
  3.1 0.1 add.29
  3.1 0.2 select_reduce_fusion.where_ref
  3.3 0.1 broadcast_in_dim.20
  3.4 0.4 copy.8.live_ref
  3.8 0.0 copy-start.2
  3.8 1.2 %copy-done.2 = bf16[512,1024]{1,0:T(8,128)(2,1)S(1)} copy-done((bf16[512,1024]{1,0:T(8,128)(2,1)S(1)}, bf16[512,1024]{1,0:T(8,128)(2,1)}, u32[]{:S(2)}) %copy-start.2) | copy-done | bytes 1048600
  5.0 0.0 copy-start.3
  5.0 1.0 %copy-done.3 = bf16[2048,128]{1,0:T(8,128)(2,1)S(1)} copy-done((bf16[2048,128]{1,0:T(8,128)(2,1)S(1)}, bf16[2048,128]{1,0:T(8,128)(2,1)}, u32[]{:S(2)}) %copy-start.3) | copy-done | bytes 524312
  6.0 54.7 %shard_map.68 = (bf16[1024,1024]{1,0:T(8,128)(2,1)}, bf16[2048,512]{1,0:T(8,128)(2,1)}, bf16[2048,512]{1,0:T(8,128)(2,1)}, f32[512,1024]{1,0:T(8,128)}, bf16[32768,128]{1,0:T(8,128)(2,1)}) custom-call(bf16[512,1024]{1,0:T(8,128)(2,1)S(1)} %copy-done.2, bf16[1024,1024]{1,0:T(8,128)(2,1)} %coup_ref.1, f32[2048,1]{1,0:T(8,128)S(1)} %copy.8.live_ref, ...), custom_call_target="tpu_custom_call" | custom-call | tf_op jit(solution)/shard_map/pallas_call | solution.py:309
  60.8 0.0 copy-start
  60.8 1.6 %copy-done = bf16[2048,512]{1,0:T(8,128)(2,1)S(1)} copy-done((bf16[2048,512]{1,0:T(8,128)(2,1)S(1)}, bf16[2048,512]{1,0:T(8,128)(2,1)}, u32[]{:S(2)}) %copy-start) | copy-done | bytes 2097176
  62.4 0.0 copy-start.1
  62.4 1.6 %copy-done.1 = bf16[2048,512]{1,0:T(8,128)(2,1)S(1)} copy-done((bf16[2048,512]{1,0:T(8,128)(2,1)S(1)}, bf16[2048,512]{1,0:T(8,128)(2,1)}, u32[]{:S(2)}) %copy-start.1) | copy-done | bytes 2097176
  63.9 15.4 %shard_map.69 = (f32[512,1024]{1,0:T(8,128)}, f32[1,512]{1,0:T(1,128)}) custom-call(s32[256]{0:T(256)S(1)} %select_reduce_fusion.where_ref, bf16[2048,512]{1,0:T(8,128)(2,1)S(1)} %copy-done, bf16[2048,512]{1,0:T(8,128)(2,1)S(1)} %copy-done.1, f32[512,1024]{1,0:T(8,128)} %get-tuple-element.10.square_ref, bf16[32768,128]{1,0:T(8,128)(2,1)} %get-tuple-element.11.pool_ref), custom_call_target="tpu_custom_call" | custom-call | tf_op jit(solution)/shard_map/pallas_call | solution.py:341
  (1 shorter events, 0.0 us)
Async XLA Ops:
  3.8 1.2 %copy-start.2 = (bf16[512,1024]{1,0:T(8,128)(2,1)S(1)}, bf16[512,1024]{1,0:T(8,128)(2,1)}, u32[]{:S(2)}) copy-start(bf16[512,1024]{1,0:T(8,128)(2,1)} %sep_ref.1) | copy-start | bytes 3145732
  5.0 1.0 %copy-start.3 = (bf16[2048,128]{1,0:T(8,128)(2,1)S(1)}, bf16[2048,128]{1,0:T(8,128)(2,1)}, u32[]{:S(2)}) copy-start(bf16[2048,128]{1,0:T(8,128)(2,1)} %anc_ref.1) | copy-start | bytes 1572868
  60.8 1.6 %copy-start = (bf16[2048,512]{1,0:T(8,128)(2,1)S(1)}, bf16[2048,512]{1,0:T(8,128)(2,1)}, u32[]{:S(2)}) copy-start(bf16[2048,512]{1,0:T(8,128)(2,1)} %get-tuple-element.8.wide_ref) | copy-start | bytes 6291460
  62.4 1.6 %copy-start.1 = (bf16[2048,512]{1,0:T(8,128)(2,1)S(1)}, bf16[2048,512]{1,0:T(8,128)(2,1)}, u32[]{:S(2)}) copy-start(bf16[2048,512]{1,0:T(8,128)(2,1)} %get-tuple-element.9.wide_other) | copy-start | bytes 6291460

commit v3 on v2

--- a/solution.py
+++ b/solution.py
@@ -35,16 +35,16 @@
     depth,
     sep_ref,
     coup_ref,
-    live_ref,
     anc_ref,
+    wide_out,
+    wide_other,
+    square_out,
+    pool_ref,
     inv_ref,
     wide_ref,
-    wide_other,
     square_ref,
-    pool_ref,
     lmat,
-    sep_other,
-    coup_other,
+    coup_all,
     xl,
     xd,
     panel_send,
@@ -117,32 +117,37 @@
         push(place(k, 3), place(k, 3), share_recv, partner)
 
     def stage(k):
+        if 2 <= k <= depth + 1:
+            finish(k - 2)
+        if 1 <= k <= depth:
+            relay(k - 1)
         if k < depth:
             open_block(k)
-        if 1 <= k <= depth:
-            relay(k - 1)
-        if 2 <= k <= depth + 1:
-            finish(k - 2)
-
-    sep_copy = remote(sep_ref, sep_other, panel_send.at[0], panel_recv.at[0], partner)
-    coup_copy = remote(coup_ref, coup_other, panel_send.at[1], panel_recv.at[1], partner)
+
+    rows = coup_ref.shape[0]
+    upper = pl.ds(pl.multiple_of(me * half, half), half)
+    sep_copy = remote(sep_ref, lmat.at[upper, :], panel_send.at[0], panel_recv.at[0], partner)
+    coup_copy = remote(coup_ref, coup_all.at[pl.ds(rows, rows), :], panel_send.at[1], panel_recv.at[1], partner)
     wide_copy = remote(wide_ref, wide_other, panel_send.at[2], panel_recv.at[2], partner)
+    sep_keep = pltpu.make_async_copy(sep_ref, lmat.at[upper, :], local_sem.at[0])
     sep_copy.start()
     for k in range(1, depth):
         push(own, place(0, 0), z_recv.at[k], peers[k - 1])
         if k == 1:
             stage(0)
     coup_copy.start()
+    sep_keep.start()
+    coup_keep = pltpu.make_async_copy(coup_ref, coup_all.at[pl.ds(0, rows), :], local_sem.at[1])
+    coup_keep.start()
     keep = pltpu.make_async_copy(
-        anc_ref, pool_ref.at[pl.ds(pl.multiple_of(group * slab, slab), slab), :], local_sem
+        anc_ref, pool_ref.at[pl.ds(pl.multiple_of(group * slab, slab), slab), :], local_sem.at[2]
     )
     keep.start()
 
-    lmat[pl.ds(pl.multiple_of(me * half, half), half), :] = sep_ref[...]
     inv_ref[...] = jnp.zeros_like(inv_ref)
     xl[...] = jnp.zeros_like(xl)
-    sep_copy.wait_recv()
-    lmat[pl.ds(pl.multiple_of((1 - me) * half, half), half), :] = sep_other[...]
+    sep_keep.wait()
+    remote(sep_ref, lmat.at[pl.ds(pl.multiple_of((1 - me) * half, half), half), :], panel_send.at[0], panel_recv.at[0], partner).wait_recv()
 
     blocks = n // DIAG
     row = lax.broadcasted_iota(jnp.int32, (DIAG, DIAG), 0)
@@ -189,21 +194,25 @@
         size *= 2
     stage(2)
 
-    rows = coup_ref.shape[0]
     chunk = min(512, rows)
     columns = pl.ds(pl.multiple_of(me * half, half), half)
+    coup_keep.wait()
     coup_copy.wait_recv()
 
-    @pl.loop(0, rows // chunk)
+    @pl.loop(0, 2 * rows // chunk)
     def _(i):
-        for source, base in ((coup_ref, 0), (coup_other, rows)):
-            take = pl.ds(pl.multiple_of(i * chunk, chunk), chunk)
-            put = pl.ds(pl.multiple_of(base + i * chunk, chunk), chunk)
-            w = mm(source[take, :], inv_ref[:, columns])
-            wide_ref[put, :] = jnp.where(live_ref[put, :] > 0, w, 0.0).astype(BF)
+        take = pl.ds(pl.multiple_of(i * chunk, chunk), chunk)
+        wide_ref[take, :] = mm(coup_all[take, :], inv_ref[:, columns]).astype(BF)
 
     stage(3)
     wide_copy.start()
+    wide_keep = pltpu.make_async_copy(wide_ref, wide_out, local_sem.at[3])
+    wide_keep.start()
+    strip = pool_ref.shape[0] - 4 * depth * slab
+    blank = pltpu.make_async_copy(
+        inv_ref.at[pl.ds(0, strip), pl.ds(n - DIAG, DIAG)], pool_ref.at[pl.ds(4 * depth * slab, strip), :], local_sem.at[4]
+    )
+    blank.start()
 
     @pl.loop(0, n // 256)
     def _(i):
@@ -212,6 +221,8 @@
             inv_ref[:, columns], inv_ref[:, take], (((0,), (0,)), ((), ())), preferred_element_type=F32
         )
 
+    square_keep = pltpu.make_async_copy(square_ref, square_out, local_sem.at[5])
+    square_keep.start()
     for k in range(4, depth + 2):
         stage(k)
 
@@ -220,107 +231,131 @@
     remote(shared, shared, out_send, share_recv, partner).wait_recv()
     sent = pool_ref.at[pl.ds(0, (2 * total) * part), :]
     remote(sent, sent, out_send, share_recv, partner).wait_send()
-    keep.wait()
+    for copy in (keep, wide_keep, blank, square_keep):
+        copy.wait()
     sep_copy.wait_send()
     coup_copy.wait_send()
     wide_copy.wait()
 
 
-def last_kernel(where_ref, wide_ref, wide_other, square_ref, pool_ref, out_ref, var_ref, sigma, sem):
+def last_kernel(
+    list_ref,
+    slot_ref,
+    wide_in,
+    other_in,
+    square_in,
+    pool_ref,
+    out_ref,
+    var_ref,
+    sigma,
+    wide,
+    wide_other,
+    carried,
+    out,
+    place,
+    tile_sem,
+    load_sem,
+    store_sem,
+):
     me = lax.axis_index("panel")
-    rows, half = wide_ref.shape
+    group = lax.axis_index("front")
+    rows, half = wide.shape
     edge = pool_ref.shape[1]
-    strips = where_ref.shape[0]
-    strip_rows = rows * rows // (strips * edge)
+    groups, slots = slot_ref.shape
+    total = groups * slots
+    strip_rows = rows * rows // (total * edge)
+    strip_count = edge // strip_rows
     across = rows // edge
-    chunks = sem.shape[0]
+    chunks = tile_sem.shape[0]
     chunk = rows // chunks
-
-    @pl.loop(0, strips)
-    def _(k):
-        source = pl.ds(pl.multiple_of(where_ref[k] * strip_rows, strip_rows), strip_rows)
-        down = pl.multiple_of((k // across) * strip_rows, strip_rows)
-        over = pl.multiple_of((k % across) * edge, edge)
-        pltpu.make_async_copy(
-            pool_ref.at[source, :],
-            sigma.at[pl.ds(down, strip_rows), pl.ds(over, edge)],
-            sem.at[k // (strips // chunks)],
-        ).start()
-
-    mine = pl.ds(pl.multiple_of(me * half, half), half)
-    other = pl.ds(pl.multiple_of((1 - me) * half, half), half)
-
-    def tmm(a, b):
-        return lax.dot_general(a, b, (((0,), (0,)), ((), ())), preferred_element_type=F32)
-
-    out_ref[...] = square_ref[...]
+    low, high = pl.ds(0, rows // 2), pl.ds(rows // 2, rows // 2)
+
+    load_wide = pltpu.make_async_copy(wide_in, wide, load_sem.at[0])
+    load_low = pltpu.make_async_copy(other_in.at[high, :], wide_other.at[low, :], load_sem.at[1])
+    load_high = pltpu.make_async_copy(other_in.at[low, :], wide_other.at[high, :], load_sem.at[2])
+    load_square = pltpu.make_async_copy(square_in, out, load_sem.at[3])
+    load_wide.start()
+
+    @pl.loop(0, groups)
+    def _(g):
+        for s in range(slots):
+            place[slot_ref[g, s]] = g * slots + s
+
+    def block(i):
+        return list_ref[group, (i + me * (across // 2)) % across]
+
+    def fetch(i):
+        a = block(i)
+        for j in range(across):
+            b = block(j)
+            live = (a >= 0) & (b >= 0)
+            for q in range(strip_count):
+                at = place[jnp.where(live, a * groups + b * strip_count + q, 0)]
+                source = pl.multiple_of(jnp.where(live, at, total) * strip_rows, strip_rows)
+                down = pl.multiple_of(i * edge + q * strip_rows, strip_rows)
+                pltpu.make_async_copy(
+                    pool_ref.at[pl.ds(source, strip_rows), :],
+                    sigma.at[pl.ds(down, strip_rows), pl.ds(j * edge, edge)],
+                    tile_sem.at[i // (across // chunks)],
+                ).start()
+
+    pl.loop(0, across)(fetch)
+    load_low.start()
+    load_high.start()
+    load_square.start()
+    load_wide.wait()
 
     @pl.loop(0, chunks)
     def _(i):
         take = pl.ds(pl.multiple_of(i * chunk, chunk), chunk)
-        turned = ((i + chunks // 2) % chunks) * chunk
-        swapped = pl.ds(pl.multiple_of(turned, chunk), chunk)
-        pltpu.make_async_copy(sigma.at[take, :], sigma.at[take, :], sem.at[i]).wait()
-        carried = mm(sigma[take, :], wide_ref[...]).astype(BF)
-        out_ref[:, mine] += tmm(carried, wide_ref[take, :])
-        out_ref[:, other] += tmm(carried, wide_other[swapped, :])
-
-    block = out_ref[:, mine]
+        pltpu.make_async_copy(sigma.at[take, :], sigma.at[take, :], tile_sem.at[i]).wait()
+        carried[:, take] = mm(sigma[take, :], wide[...]).T.astype(BF)
+
+    load_low.wait()
+    load_high.wait()
+    load_square.wait()
+    step = 256
+    for source, base in ((wide, me), (wide_other, 1 - me)):
+        for c in range(half // step):
+            put = pl.ds(pl.multiple_of(base * half + c * step, step), step)
+            out[:, put] += mm(carried[...], source[:, pl.ds(c * step, step)])
+            pltpu.make_async_copy(out.at[:, put], out_ref.at[:, put], store_sem).start()
+    block_out = out[:, pl.ds(pl.multiple_of(me * half, half), half)]
     row = lax.broadcasted_iota(jnp.int32, (half, half), 0)
     col = lax.broadcasted_iota(jnp.int32, (half, half), 1)
-    var_ref[...] = jnp.sum(jnp.where(row == col, block, 0.0), axis=0, keepdims=True)
+    var_ref[...] = jnp.sum(jnp.where(row == col, block_out, 0.0), axis=0, keepdims=True)
+    pltpu.make_async_copy(out, out_ref, store_sem).wait()
 
 
 def on_device(sep_factor, coup_factor, coup_list, slot_tiles, anc_tiles):
     panels = lax.axis_size("panel")
     groups = lax.axis_size("front")
-    me = lax.axis_index("panel")
-    my_group = lax.axis_index("front")
     half, width = sep_factor.shape
     edge = anc_tiles.shape[1]
     slots = slot_tiles.shape[1]
     strip_rows = anc_tiles.shape[0] // slots
-    strip_count = edge // strip_rows
-    list_width = coup_list.shape[1]
-    row_blocks = list_width // panels
-    rows = list_width * edge
+    rows = coup_list.shape[1] * edge
     vmem = pl.BlockSpec(memory_space=pltpu.VMEM)
-    hbm = pl.BlockSpec(memory_space=pl.ANY)
-
-    own_list = coup_list[my_group]
-    own_list = jnp.where(me == 0, own_list, jnp.roll(own_list, -row_blocks))
-    live = jnp.repeat((own_list >= 0).astype(F32), edge)[:, None]
-    blocks = jnp.maximum(own_list, 0)
-    wanted = (
-        blocks[:, None, None] * groups
-        + jnp.arange(strip_count, dtype=jnp.int32)[None, :, None]
-        + blocks[None, None, :] * strip_count
-    ).reshape(-1)
-    flat = slot_tiles.reshape(-1)
-    place = jnp.sum(
-        jnp.where(
-            wanted[:, None] == flat[None, :], jnp.arange(flat.shape[0], dtype=jnp.int32)[None, :], 0
-        ),
-        axis=1,
-    )
-
+    smem = pl.BlockSpec(memory_space=pltpu.SMEM)
+    hbm = pl.BlockSpec(memory_space=pltpu.HBM)
     depth = groups // 4
     dma = pltpu.SemaphoreType.DMA
-    _, wide, wide_other, square, pool = pl.pallas_call(
+    wide, wide_other, square, pool = pl.pallas_call(
         functools.partial(first_kernel, depth),
         out_shape=(
-            jax.ShapeDtypeStruct((width, width), BF),
             jax.ShapeDtypeStruct((rows, half), BF),
             jax.ShapeDtypeStruct((rows, half), BF),
             jax.ShapeDtypeStruct((half, width), F32),
-            jax.ShapeDtypeStruct((groups * anc_tiles.shape[0], edge), BF),
+            jax.ShapeDtypeStruct((groups * anc_tiles.shape[0] + strip_rows, edge), BF),
         ),
-        in_specs=[vmem] * 3 + [hbm],
-        out_specs=[vmem] * 4 + [hbm],
+        in_specs=[hbm] * 3,
+        out_specs=[hbm] * 4,
         scratch_shapes=[
             pltpu.VMEM((width, width), BF),
-            pltpu.VMEM((half, width), BF),
-            pltpu.VMEM((rows // panels, width), BF),
+            pltpu.VMEM((rows, half), BF),
+            pltpu.VMEM((half, width), F32),
+            pltpu.VMEM((width, width), BF),
+            pltpu.VMEM((rows, width), BF),
             pltpu.VMEM((width, width), BF),
             pltpu.VMEM((width // DIAG, DIAG, DIAG), F32),
             dma((3,)),
@@ -332,23 +367,33 @@
             dma((depth,)),
             dma,
             dma,
-            dma,
+            dma((6,)),
         ],
         compiler_params=pltpu.CompilerParams(
             vmem_limit_bytes=48 << 20, collective_id=0, has_side_effects=True
         ),
-    )(sep_factor, coup_factor, live, anc_tiles)
+    )(sep_factor, coup_factor, anc_tiles)
     selected, variances = pl.pallas_call(
         last_kernel,
         out_shape=(
             jax.ShapeDtypeStruct((half, width), F32),
             jax.ShapeDtypeStruct((1, half), F32),
         ),
-        in_specs=[pl.BlockSpec(memory_space=pltpu.SMEM), vmem, vmem, vmem, hbm],
-        out_specs=[vmem] * 2,
-        scratch_shapes=[pltpu.VMEM((rows, rows), BF), dma((4,))],
+        in_specs=[smem, smem] + [hbm] * 4,
+        out_specs=[hbm, vmem],
+        scratch_shapes=[
+            pltpu.VMEM((rows, rows), BF),
+            pltpu.VMEM((rows, half), BF),
+            pltpu.VMEM((rows, half), BF),
+            pltpu.VMEM((half, rows), BF),
+            pltpu.VMEM((half, width), F32),
+            pltpu.SMEM((groups * slots,), jnp.int32),
+            dma((4,)),
+            dma((4,)),
+            dma,
+        ],
         compiler_params=pltpu.CompilerParams(vmem_limit_bytes=48 << 20),
-    )(place, wide, wide_other, square, pool)
+    )(coup_list, slot_tiles, wide, wide_other, square, pool)
     return selected, variances.reshape(half)
 
 

time: 80.7 us -> 69.8 us (0.86); the launches traced: 79.4 us -> 70.7 us
  local copies, waits for them, and re-layouts: 7.51 us -> 2.27 us
  Pallas kernels: 70.1 us -> 67.8 us
  other arithmetic: 1.05 us -> 0 us
    pallas_call x1, Pallas kernels: 54.7 us -> 51.5 us  [on_device(): pl.pallas_call(functools.partial(first_kernel, depth), out_shape=(jax.Sha...]
    unnamed x8, local copies, waits for them, and re-layouts: 5.44 us -> 2.27 us
    pallas_call x1, Pallas kernels: 15.4 us -> 16.3 us  [on_device(): pl.pallas_call(last_kernel, out_shape=(jax.ShapeDtypeStruct((half, width)...]
where the time goes in v3:
time: 69.8 us; the launch traced here: 70.7 us
  Pallas kernels  67.8 us (97%)
  local copies, waits for them, and re-layouts  2.27 us (3%)
    pallas_call x1, Pallas kernels, on_device(): pl.pallas_call(functools.partial(first_kernel, depth), out_shape=(jax.Sha...  51.5 us
    pallas_call x1, Pallas kernels, on_device(): pl.pallas_call(last_kernel, out_shape=(jax.ShapeDtypeStruct((half, width)...  16.3 us
    unnamed x8, local copies, waits for them, and re-layouts  2.27 us

profile of v3, /device:TPU:0, one launch (start us, length us, event | category | flops | bytes accessed | tf_op | source)
XLA Modules:
  0.0 70.7 jit_solution(3118371604801680968)
XLA Ops:
  0.6 0.0 copy-start
  0.6 1.2 %copy-done = bf16[512,1024]{1,0:T(8,128)(2,1)S(1)} copy-done((bf16[512,1024]{1,0:T(8,128)(2,1)S(1)}, bf16[512,1024]{1,0:T(8,128)(2,1)}, u32[]{:S(2)}) %copy-start) | copy-done | bytes 1048600
  1.9 0.0 copy-start.1
  1.9 1.0 %copy-done.1 = bf16[2048,128]{1,0:T(8,128)(2,1)S(1)} copy-done((bf16[2048,128]{1,0:T(8,128)(2,1)S(1)}, bf16[2048,128]{1,0:T(8,128)(2,1)}, u32[]{:S(2)}) %copy-start.1) | copy-done | bytes 524312
  2.9 0.0 copy-start.2
  2.9 0.0 copy-start.3
  2.9 51.5 %shard_map.68 = (bf16[2048,512]{1,0:T(8,128)(2,1)S(1)}, bf16[2048,512]{1,0:T(8,128)(2,1)S(1)}, f32[512,1024]{1,0:T(8,128)}, bf16[32896,128]{1,0:T(8,128)(2,1)}) custom-call(bf16[512,1024]{1,0:T(8,128)(2,1)S(1)} %copy-done, bf16[1024,1024]{1,0:T(8,128)(2,1)} %coup_ref.1, bf16[2048,128]{1,0:T(8,128)(2,1)S(1)} %copy-done.1), custom_call_target="tpu_custom_call" | custom-call | tf_op jit(solution)/shard_map/pallas_call | solution.py:343
  54.4 0.0 copy-done.2
  54.4 0.0 copy-done.3
  54.4 16.3 %shard_map.69 = (f32[512,1024]{1,0:T(8,128)}, f32[1,512]{1,0:T(1,128)}) custom-call(s32[16,16]{1,0:T(8,128)S(1)} %copy-done.2, s32[16,16]{1,0:T(8,128)S(1)} %copy-done.3, bf16[2048,512]{1,0:T(8,128)(2,1)S(1)} %get-tuple-element.8.wide_in, bf16[2048,512]{1,0:T(8,128)(2,1)S(1)} %get-tuple-element.9.other_in, f32[512,1024]{1,0:T(8,128)} %get-tuple-element.10.square_in, ...), custom_call_target="tpu_custom_call" | custom-call | tf_op jit(solution)/shard_map/pallas_call | solution.py:376
Async XLA Ops:
  0.6 1.2 %copy-start = (bf16[512,1024]{1,0:T(8,128)(2,1)S(1)}, bf16[512,1024]{1,0:T(8,128)(2,1)}, u32[]{:S(2)}) copy-start(bf16[512,1024]{1,0:T(8,128)(2,1)} %sep_ref.1) | copy-start | bytes 3145732
  1.9 1.0 %copy-start.1 = (bf16[2048,128]{1,0:T(8,128)(2,1)S(1)}, bf16[2048,128]{1,0:T(8,128)(2,1)}, u32[]{:S(2)}) copy-start(bf16[2048,128]{1,0:T(8,128)(2,1)} %anc_ref.1) | copy-start | bytes 1572868
  2.9 51.5 %copy-start.2 = (s32[16,16]{1,0:T(8,128)S(1)}, s32[16,16]{1,0:T(8,128)}, u32[]{:S(2)}) copy-start(s32[16,16]{1,0:T(8,128)} %list_ref.1) | copy-start | bytes 3076
  2.9 51.5 %copy-start.3 = (s32[16,16]{1,0:T(8,128)S(1)}, s32[16,16]{1,0:T(8,128)}, u32[]{:S(2)}) copy-start(s32[16,16]{1,0:T(8,128)} %slot_ref.1) | copy-start | bytes 3076

commit v4 on v3

--- a/solution.py
+++ b/solution.py
@@ -370,7 +370,7 @@
             dma((6,)),
         ],
         compiler_params=pltpu.CompilerParams(
-            vmem_limit_bytes=48 << 20, collective_id=0, has_side_effects=True
+            vmem_limit_bytes=63 << 20, collective_id=0, has_side_effects=True
         ),
     )(sep_factor, coup_factor, anc_tiles)
     selected, variances = pl.pallas_call(
@@ -392,7 +392,7 @@
             dma((4,)),
             dma,
         ],
-        compiler_params=pltpu.CompilerParams(vmem_limit_bytes=48 << 20),
+        compiler_params=pltpu.CompilerParams(vmem_limit_bytes=63 << 20),
     )(coup_list, slot_tiles, wide, wide_other, square, pool)
     return selected, variances.reshape(half)
 

time: 69.8 us -> 68.8 us (0.986)
  local copies, waits for them, and re-layouts: 2.27 us -> 0 us
  Pallas kernels: 67.8 us -> 68.8 us
    unnamed x8 -> x0, local copies, waits for them, and re-layouts: 2.27 us -> none
    pallas_call x1, Pallas kernels: 16.3 us -> 17.4 us  [on_device(): pl.pallas_call(last_kernel, out_shape=(jax.ShapeDtypeStruct((half, width)...]
where the time goes in v4:
time: 68.8 us; the launch traced here: 69.4 us
  Pallas kernels  68.8 us (100%)
    pallas_call x1, Pallas kernels, on_device(): pl.pallas_call(functools.partial(first_kernel, depth), out_shape=(jax.Sha...  51.4 us
    pallas_call x1, Pallas kernels, on_device(): pl.pallas_call(last_kernel, out_shape=(jax.ShapeDtypeStruct((half, width)...  17.4 us

profile of v4, /device:TPU:0, one launch (start us, length us, event | category | flops | bytes accessed | tf_op | source)
XLA Modules:
  0.0 69.4 jit_solution(16538700593381313169)
XLA Ops:
  0.6 51.4 %shard_map.68 = (bf16[2048,512]{1,0:T(8,128)(2,1)}, bf16[2048,512]{1,0:T(8,128)(2,1)}, f32[512,1024]{1,0:T(8,128)}, bf16[32896,128]{1,0:T(8,128)(2,1)}) custom-call(bf16[512,1024]{1,0:T(8,128)(2,1)} %sep_ref.1, bf16[1024,1024]{1,0:T(8,128)(2,1)} %coup_ref.1, bf16[2048,128]{1,0:T(8,128)(2,1)} %anc_ref.1), custom_call_target="tpu_custom_call" | custom-call | tf_op jit(solution)/shard_map/pallas_call | solution.py:343
  52.0 17.4 %shard_map.69 = (f32[512,1024]{1,0:T(8,128)}, f32[1,512]{1,0:T(1,128)}) custom-call(s32[16,16]{1,0:T(8,128)} %list_ref.1, s32[16,16]{1,0:T(8,128)} %slot_ref.1, bf16[2048,512]{1,0:T(8,128)(2,1)} %get-tuple-element.8.wide_in, bf16[2048,512]{1,0:T(8,128)(2,1)} %get-tuple-element.9.other_in, f32[512,1024]{1,0:T(8,128)} %get-tuple-element.10.square_in, ...), custom_call_target="tpu_custom_call" | custom-call | tf_op jit(solution)/shard_map/pallas_call | solution.py:376

commit v5 on v4

--- a/solution.py
+++ b/solution.py
@@ -96,17 +96,29 @@
         source = own if k == 0 else place(k, 0)
         if k > 0:
             arrived(source, z_recv.at[k])
-        push(source, place(k, 0), x_recv.at[k], beside)
-        push(source, place(k, 0), y_recv.at[k], behind)
+        piece = part // 2
+        for first in (True, False):
+            for recv, device, low in (
+                (x_recv, beside, piece if first else 0),
+                (y_recv, behind, 0 if first else piece),
+            ):
+                push(
+                    source.at[pl.ds(low, piece), :],
+                    place(k, 0, low, piece),
+                    recv.at[k if first else depth + k],
+                    device,
+                )
         if k > 0:
             push(source, source, share_recv, partner)
 
     def relay(k):
         piece = part // 2
-        arrived(place(k, 1), x_recv.at[k])
+        arrived(place(k, 1, piece, piece), x_recv.at[k])
         push(place(k, 1, piece, piece), place(k, 1, piece, piece), second_recv.at[k], behind)
-        arrived(place(k, 2), y_recv.at[k])
+        arrived(place(k, 2, 0, piece), y_recv.at[k])
         push(place(k, 2, 0, piece), place(k, 2, 0, piece), first_recv.at[k], beside)
+        arrived(place(k, 1, 0, piece), x_recv.at[depth + k])
+        arrived(place(k, 2, piece, piece), y_recv.at[depth + k])
         push(place(k, 1), place(k, 1), share_recv, partner)
         push(place(k, 2), place(k, 2), share_recv, partner)
 
@@ -361,8 +373,8 @@
             dma((3,)),
             dma((3,)),
             dma((depth,)),
-            dma((depth,)),
-            dma((depth,)),
+            dma((2 * depth,)),
+            dma((2 * depth,)),
             dma((depth,)),
             dma((depth,)),
             dma,

time: 68.8 us -> 65.8 us (0.956)
  the two profiles are of different devices: /device:TPU:0 before, /device:TPU:1 now
where the time goes in v5:
time: 65.8 us; the launch traced here: 66.5 us
  Pallas kernels  65.8 us (100%)
    pallas_call x1, Pallas kernels, on_device(): pl.pallas_call(functools.partial(first_kernel, depth), out_shape=(jax.Sha...  48.5 us
    pallas_call x1, Pallas kernels, on_device(): pl.pallas_call(last_kernel, out_shape=(jax.ShapeDtypeStruct((half, width)...  17.3 us

profile of v5, /device:TPU:1, one launch (start us, length us, event | category | flops | bytes accessed | tf_op | source)
XLA Modules:
  0.0 66.5 jit_solution(8174122060149237447)
XLA Ops:
  0.6 48.5 %shard_map.68 = (bf16[2048,512]{1,0:T(8,128)(2,1)}, bf16[2048,512]{1,0:T(8,128)(2,1)}, f32[512,1024]{1,0:T(8,128)}, bf16[32896,128]{1,0:T(8,128)(2,1)}) custom-call(bf16[512,1024]{1,0:T(8,128)(2,1)} %sep_ref.1, bf16[1024,1024]{1,0:T(8,128)(2,1)} %coup_ref.1, bf16[2048,128]{1,0:T(8,128)(2,1)} %anc_ref.1), custom_call_target="tpu_custom_call" | custom-call | tf_op jit(solution)/shard_map/pallas_call | solution.py:355
  49.1 17.3 %shard_map.69 = (f32[512,1024]{1,0:T(8,128)}, f32[1,512]{1,0:T(1,128)}) custom-call(s32[16,16]{1,0:T(8,128)} %list_ref.1, s32[16,16]{1,0:T(8,128)} %slot_ref.1, bf16[2048,512]{1,0:T(8,128)(2,1)} %get-tuple-element.8.wide_in, bf16[2048,512]{1,0:T(8,128)(2,1)} %get-tuple-element.9.other_in, f32[512,1024]{1,0:T(8,128)} %get-tuple-element.10.square_in, ...), custom_call_target="tpu_custom_call" | custom-call | tf_op jit(solution)/shard_map/pallas_call | solution.py:388
